TPU v7x, 32 devices: a whole 2x2x4 slice. The times are simulated.
32 devices in a mesh: grp: 2 (over x), res: 16 (over z, y, core).
Axes of the slice: x: 2, y: 2, z: 4, core: 2. Of those that a mesh axis runs over, the one named last changes fastest.
Arguments:
- alignment_activations: bfloat16 [128, 128, 256], P('grp', 'res'), parts along dimension 0, may hold values from -6 to 6
- projection_weight: bfloat16 [256, 64], replicated, may hold values from -0.375 to 0.375
- output_weight: bfloat16 [1024, 128], replicated, may hold values from -0.1875 to 0.1875
- output_bias: float32 [128], replicated, may hold values from -3 to 3
- pair_update_gradient: bfloat16 [256, 128, 128], P(('grp', 'res')), parts along dimension 0, may hold values from -6 to 6
- sequence_mask: int32 [128], P('grp'), parts along dimension 0, may hold values 0 or 1
- residue_mask: int32 [256], P('grp'), parts along dimension 0, may hold values 0 or 1
Outputs:
- pair_increment: bfloat16 [256, 128, 128], P(('grp', 'res')), parts along dimension 0
- alignment_gradient: bfloat16 [128, 128, 256], P('grp', 'res'), parts along dimension 0
There are 2 independent parts, one for each index of `grp`. A program takes and returns all parts, laid end to end along the dimension named above; an argument that names none is the same for every part. Nothing has to cross between parts.
All inputs are finite; a program needn't handle non-finite values.
Results may differ from a plain program's by a relative error of at most 0.007.
Values may be sent and summed in bfloat16 or wider, within the bound.
No kernel may reach another device: no remote copies, remote signals or barrier semaphores. Data moves between devices by JAX's collectives and lax.ppermute only.
A program may use at most 64 MiB of HBM per device.

v0:
```python
import jax
import jax.numpy as jnp
from jax import lax
from jax.sharding import PartitionSpec as P

eps_norm = 1e-05


def layer_norm_forward(values):
    mean_val = jnp.mean(values, axis=-1, keepdims=True)
    centered = values - mean_val
    inverse_deviation = lax.rsqrt(jnp.mean(centered * centered, axis=-1, keepdims=True) + eps_norm)
    return (centered * inverse_deviation, inverse_deviation)


def layer_norm_backward(grad_out, scaled_product, inverse_deviation):
    mean_grad = jnp.mean(grad_out, axis=-1, keepdims=True)
    mean_cross = jnp.mean(grad_out * scaled_product, axis=-1, keepdims=True)
    return inverse_deviation * (grad_out - mean_grad - scaled_product * mean_cross)


def body(
    alignment_activations,
    projection_weight,
    output_weight,
    output_bias,
    pair_update_gradient,
    sequence_mask,
    residue_mask,
):
    alignment_rows = alignment_activations.shape[0]
    local_rows = alignment_activations.shape[1]
    alignment_width = alignment_activations.shape[2]
    projected_width = projection_weight.shape[1] // 2
    pair_width = output_weight.shape[1]
    row_start = lax.axis_index("res") * local_rows
    residue_float_mask = residue_mask.astype(jnp.float32)
    local_residues = lax.dynamic_slice_in_dim(residue_float_mask, row_start, local_rows)
    alignment_mask = sequence_mask.astype(jnp.float32)[:, None] * local_residues[None, :]
    scaled_product, inverse_deviation = layer_norm_forward(
        alignment_activations.astype(jnp.float32)
    )
    normalized_input = scaled_product.astype(jnp.bfloat16)
    projected_rows = jnp.dot(
        normalized_input.reshape(-1, alignment_width),
        projection_weight,
        preferred_element_type=jnp.float32,
    )
    projected_rows = (
        projected_rows.reshape(alignment_rows, local_rows, 2 * projected_width)
        * alignment_mask[:, :, None]
    )
    projected_rows = projected_rows.astype(jnp.bfloat16)
    left_projected = projected_rows[:, :, :projected_width]
    right_proj = projected_rows[:, :, projected_width:]
    live_rows = jnp.sum(sequence_mask.astype(jnp.float32))
    right_all = lax.all_gather(right_proj, "res", axis=1, tiled=True)
    residue_count = right_all.shape[1]
    block_columns = 256 if residue_count % 256 == 0 else residue_count
    block_count = residue_count // block_columns
    count_rows = jnp.maximum(live_rows * local_residues[:, None] * residue_float_mask[None, :], 1.0)

    def pair_block(carry, block_id):
        pair_increment, left_gradient, gradient_pieces = carry
        column_offset = block_id * block_columns
        right_blk = lax.dynamic_slice_in_dim(right_all, column_offset, block_columns, 1)
        cot_blk = lax.dynamic_slice_in_dim(pair_update_gradient, column_offset, block_columns, 1)
        count_blk = lax.dynamic_slice_in_dim(count_rows, column_offset, block_columns, 1)
        outer = jnp.einsum(
            "sic,sjd->ijcd", left_projected, right_blk, preferred_element_type=jnp.float32
        )
        outer = outer.astype(jnp.bfloat16).reshape(-1, projected_width * projected_width)
        update = jnp.dot(outer, output_weight, preferred_element_type=jnp.float32)
        update = update.reshape(local_rows, block_columns, pair_width) + output_bias
        update = (update / count_blk[:, :, None]).astype(jnp.bfloat16)
        pair_increment = lax.dynamic_update_slice_in_dim(pair_increment, update, column_offset, 1)
        grad_outer = jnp.dot(
            cot_blk.reshape(-1, pair_width), output_weight.T, preferred_element_type=jnp.float32
        )
        grad_outer = (
            grad_outer.reshape(local_rows, block_columns, projected_width, projected_width)
            / count_blk[:, :, None, None]
        )
        grad_outer = grad_outer.astype(jnp.bfloat16)
        left_gradient = left_gradient + jnp.einsum(
            "ijcd,sjd->sic", grad_outer, right_blk, preferred_element_type=jnp.float32
        )
        gradient_piece = jnp.einsum(
            "ijcd,sic->jsd", grad_outer, left_projected, preferred_element_type=jnp.float32
        )
        gradient_pieces = lax.dynamic_update_slice_in_dim(
            gradient_pieces,
            gradient_piece.reshape(block_columns, alignment_rows * projected_width),
            column_offset,
            0,
        )
        return ((pair_increment, left_gradient, gradient_pieces), None)

    start_update = jnp.zeros((local_rows, residue_count, pair_width), jnp.bfloat16)
    initial_left = jnp.zeros((alignment_rows, local_rows, projected_width), jnp.float32)
    initial_pieces = jnp.zeros((residue_count, alignment_rows * projected_width), jnp.float32)
    (pair_increment, left_gradient, gradient_pieces), unused = lax.scan(
        pair_block, (start_update, initial_left, initial_pieces), jnp.arange(block_count)
    )
    gradient_total = lax.psum_scatter(gradient_pieces, "res", scatter_dimension=0, tiled=True)
    right_gradient = gradient_total.reshape(local_rows, alignment_rows, projected_width).transpose(
        1, 0, 2
    )
    projection_gradient = (
        jnp.concatenate([left_gradient, right_gradient], axis=-1) * alignment_mask[:, :, None]
    )
    projection_gradient = projection_gradient.astype(jnp.bfloat16)
    normalized_gradient = jnp.dot(
        projection_gradient.reshape(-1, 2 * projected_width),
        projection_weight.T,
        preferred_element_type=jnp.float32,
    )
    normalized_gradient = normalized_gradient.reshape(alignment_rows, local_rows, alignment_width)
    alignment_gradient = layer_norm_backward(
        normalized_gradient, scaled_product, inverse_deviation
    ).astype(jnp.bfloat16)
    return (pair_increment, alignment_gradient)


def solution(mesh):
    in_specs = (
        P("grp", "res", None),
        P(),
        P(),
        P(),
        P(("grp", "res"), None, None),
        P("grp"),
        P("grp"),
    )
    out_specs = (P(("grp", "res"), None, None), P("grp", "res", None))
    return jax.shard_map(body, mesh=mesh, in_specs=in_specs, out_specs=out_specs, check_vma=False)
```

profile of v0, /device:TPU:0, one launch (start us, length us, event | category | flops | bytes accessed | tf_op | source)
XLA Modules:
  0.0 89.6 jit_solution(17013610262894951195)
XLA Ops:
  7.2 0.0 copy-start
  7.2 0.0 reduce-scatter.4.cloned.1.call-start
  7.2 1.3 %convert_reduce_fusion.1 = f32[]{:T(128)} fusion(s32[64]{0:T(128)} %param.12), kind=kLoop, calls=%fused_computation.46 | loop fusion | flops 127 | bytes 260 | tf_op jit(solution)/shard_map/reduce_sum | solution.py:56
  8.5 0.7 convert_element_type.41
  9.2 0.7 convert_element_type.42
  9.9 1.1 %convert_reduce_fusion = f32[64,8]{1,0:T(8,128)S(1)} fusion(bf16[64,8,256]{2,1,0:T(8,128)(2,1)} %param.7), kind=kLoop, calls=%fused_computation.15 | loop fusion | flops 261632 | bytes 264192 | tf_op jit(solution)/shard_map/reduce_sum | solution.py:10
  11.0 1.2 %fusion.23 = f32[64,8]{1,0:T(8,128)S(1)} fusion(bf16[64,8,256]{2,1,0:T(8,128)(2,1)} %param.7, f32[64,8]{1,0:T(8,128)S(1)} %broadcast_multiply_fusion.3), kind=kLoop, calls=%fused_computation.25 | loop fusion | flops 523776 | bytes 266240 | tf_op jit(solution)/shard_map/reduce_sum | solution.py:12
  12.2 0.7 broadcast_multiply_fusion.4
  12.9 0.1 add_rsqrt_fusion
  13.0 0.6 copy-done.4
  13.6 1.3 %fusion.9 = bf16[64,8,64]{2,1,0:T(8,128)(2,1)S(1)} fusion(bf16[64,8,256]{2,1,0:T(8,128)(2,1)} %param.7, f32[64,8]{1,0:T(8,128)S(1)} %get-tuple-element.29, f32[64,8]{1,0:T(8,128)S(1)} %broadcast_multiply_fusion.3, f32[64,8]{1,0:T(8,128)S(1)} %get-tuple-element.40, bf16[256,64]{0,1:T(8,128)(2,1)} %param.8), kind=kOutput, calls=%fused_computation.11 | convolution fusion | flops 17367040 | bytes 366592 | tf_op jit(solution)/shard_map/dot_general | solution.py:44
  14.8 0.1 fusion.39
  14.9 0.1 copy.23
  15.1 0.1 multiply_maximum_fusion
  15.2 0.7 divide_convert_fusion
  15.9 0.8 fusion.4
  16.7 0.6 copy.30
  17.3 1.3 %copy.43 = f32[128,2048]{1,0:T(8,128)} copy(f32[128,2048]{0,1:T(8,128)S(1)} %bitcast.49) | data formatting | bytes 2097152
  18.6 0.0 reduce-scatter.4.cloned.1.call-update
  18.7 32.3 %all_gather.3 = bf16[64,128,32]{2,1,0:T(8,128)(2,1)S(1)} all-gather(bf16[64,8,32]{2,1,0:T(8,128)(2,1)S(1)} %get-tuple-element.27), channel_id=1, replica_groups=mesh['grp'=2,'res'=16] {'res'}, dimensions={1}, use_global_device_ids=true | all-gather | bytes 557056 | tf_op jit(solution)/shard_map/all_gather | solution.py:57
  51.0 3.2 %copy.26 = bf16[64,128,32]{0,1,2:T(8,128)(2,1)S(1)} copy(bf16[64,128,32]{2,1,0:T(8,128)(2,1)S(1)} %all_gather.3) | data formatting | bytes 1048576 | tf_op jit(solution)/shard_map/all_gather | solution.py:57
  54.1 3.0 %fusion.10 = f32[64,8,32]{0,2,1:T(8,128)} fusion(bf16[8,128,32,32]{1,3,2,0:T(8,128)(2,1)} %copy-done.2, bf16[64,128,32]{0,1,2:T(8,128)(2,1)S(1)} %copy.26), kind=kOutput, calls=%fused_computation.12 | convolution fusion | flops 134217728 | bytes 2686976 | tf_op jit(solution)/shard_map/while/body/eval_jaxpr/ijcd,sjd->sic/dot_general | solution.py:85
  57.1 1.7 %copy.33 = f32[64,8,32]{2,1,0:T(8,128)} copy(f32[64,8,32]{0,2,1:T(8,128)} %fusion.10) | data formatting | bytes 131072 | tf_op jit(solution)/shard_map/while/body/eval_jaxpr/ijcd,sjd->sic/dot_general | solution.py:85
  58.9 3.2 %copy.34 = bf16[64,128,32,1]{0,1,3,2:T(8,128)(2,1)S(1)} copy(bf16[64,128,32,1]{2,1,0,3:T(8,128)(2,1)S(1)} %bitcast.47) | data formatting | bytes 1048576 | tf_op jit(solution)/shard_map/all_gather | solution.py:57
  62.1 0.7 convert_bitcast_fusion
  62.8 1.4 %copy.24 = bf16[8,128,32,32]{1,3,2,0:T(8,128)(2,1)S(1)} copy(bf16[8,128,32,32]{1,2,0,3:T(8,128)(2,1)S(1)} %convert_bitcast_fusion) | data formatting | bytes 4194304 | tf_op jit(solution)/shard_map/while/body/eval_jaxpr/convert_element_type | solution.py:72
  64.2 1.5 %fusion.8 = bf16[8,128,128]{2,1,0:T(8,128)(2,1)} fusion(bf16[8,128,1024]{1,2,0:T(8,128)(2,1)S(1)} %bitcast.50, bf16[1024,128]{1,0:T(8,128)(2,1)S(1)} %copy-done, f32[8,128]{1,0:T(8,128)S(1)} %multiply_maximum_fusion, f32[128]{0:T(128)S(1)} %copy-done.8), kind=kOutput, calls=%fused_computation.9 | convolution fusion | flops 268828672 | bytes 2626048 | tf_op jit(solution)/shard_map/while/body/eval_jaxpr/dot_general | solution.py:73
  65.7 14.0 %reduce-scatter.4.cloned.1.call-done = f32[8,2048]{1,0:T(8,128)} async-done(((f32[128,2048]{1,0:T(8,128)}), f32[8,2048]{1,0:T(8,128)}) %reduce-scatter.4.cloned.1.call-update) | async-done | bytes 65552
  79.7 1.2 %copy.44 = f32[8,2048]{0,1:T(8,128)S(1)} copy(f32[8,2048]{1,0:T(8,128)} %reduce-scatter.4.cloned.1.call-done) | data formatting | bytes 131072
  80.9 0.3 copy.32
  81.2 0.5 fusion.38
  81.8 1.0 %fusion.22 = bf16[64,8,256]{2,1,0:T(8,128)(2,1)} fusion(bf16[64,8,256]{2,1,0:T(8,128)(2,1)S(1)} %copy-done.1, f32[64,8,256]{2,1,0:T(8,128)S(1)} %get-tuple-element.28, f32[64,8]{1,0:T(8,128)S(1)} %broadcast_multiply_fusion.1, f32[64,8]{1,0:T(8,128)S(1)} %broadcast_multiply_fusion.2, f32[64,8]{1,0:T(8,128)S(1)} %get-tuple-element.29, ...), kind=kLoop, calls=%fused_computation.24 | loop fusion | flops 1048576 | bytes 1056768 | tf_op jit(solution)/shard_map/convert_element_type | solution.py:121
  (19 shorter events, 0.0 us)
Async XLA Ops:
  7.2 8.0 %copy-start = (bf16[1024,128]{1,0:T(8,128)(2,1)S(1)}, bf16[1024,128]{1,0:T(8,128)(2,1)}, u32[]{:S(2)}) copy-start(bf16[1024,128]{1,0:T(8,128)(2,1)} %param.9) | copy-start | bytes 786436
  7.2 8.0 %copy-start.7 = (bf16[8,128,128]{2,1,0:T(8,128)(2,1)S(1)}, bf16[8,128,128]{2,1,0:T(8,128)(2,1)}, u32[]{:S(2)}) copy-start(bf16[8,128,128]{2,1,0:T(8,128)(2,1)} %param.11) | copy-start | bytes 786436
  7.2 72.5 %reduce-scatter.4.cloned.1.call-start = ((), (), s32[]{:S(2)}) async-start(), calls=%async_computation.1 | async-start | bytes 1114112
  13.0 0.6 copy-start.4
  15.9 1.4 %copy-start.2 = (bf16[8,128,32,32]{1,3,2,0:T(8,128)(2,1)}, bf16[8,128,32,32]{1,3,2,0:T(8,128)(2,1)S(1)}, u32[]{:S(2)}) copy-start(bf16[8,128,32,32]{1,3,2,0:T(8,128)(2,1)S(1)} %divide_convert_fusion) | copy-start | bytes 6291460
  62.8 1.4 %copy-start.8 = (f32[128]{0:T(128)S(1)}, f32[128]{0:T(128)}, u32[]{:S(2)}) copy-start(f32[128]{0:T(128)} %param.10) | copy-start | bytes 1540
  65.6 15.5 %copy-start.1 = (bf16[64,8,256]{2,1,0:T(8,128)(2,1)S(1)}, bf16[64,8,256]{2,1,0:T(8,128)(2,1)}, u32[]{:S(2)}) copy-start(bf16[64,8,256]{2,1,0:T(8,128)(2,1)} %param.7) | copy-start | bytes 786436
  65.7 15.5 %copy-start.3 = (f32[64,8,32]{2,1,0:T(8,128)S(1)}, f32[64,8,32]{2,1,0:T(8,128)}, u32[]{:S(2)}) copy-start(f32[64,8,32]{2,1,0:T(8,128)} %copy.33) | copy-start | bytes 196612
  65.7 15.5 %copy-start.5 = (f32[64,8]{1,0:T(8,128)S(1)}, f32[64,8]{1,0:T(8,128)}, u32[]{:S(2)}) copy-start(f32[64,8]{1,0:T(8,128)} %copy-done.4) | copy-start | bytes 6148
  65.7 15.6 %copy-start.6 = (bf16[256,64]{0,1:T(8,128)(2,1)S(1)}, bf16[256,64]{0,1:T(8,128)(2,1)}, u32[]{:S(2)}) copy-start(bf16[256,64]{0,1:T(8,128)(2,1)} %param.8) | copy-start | bytes 98308
Sparse Core Ops, SparseCore 0:
  18.8 60.8 reduce-scatter.3
where the time goes:
time: 90 us; the launch traced here: 89.6 us
  blocking collectives  32.3 us (36%)
  between operations  14.2 us (16%)
  waiting for transfers between devices  14 us (16%)
  local copies, waits for them, and re-layouts  13.8 us (15%)
  matrix products  8.48 us (9%)
  other arithmetic  6.82 us (8%)
    all_gather x1, blocking collectives, body(): right_all = lax.all_gather(right_proj, 'res', axis=1, tiled=True)  32.3 us
    unnamed x2, waiting for transfers between devices  14 us
    all_gather x2, local copies, waits for them, and re-layouts, body(): right_all = lax.all_gather(right_proj, 'res', axis=1, tiled=True)  6.35 us
    unnamed x20, local copies, waits for them, and re-layouts  3.13 us
    dot_general x1, matrix products, pair_block(): jnp.einsum('ijcd,sjd->sic', grad_outer, right_blk, preferred_element_type...  2.99 us
  transfers between devices with their start and end apart: 1, of which 1 were waited for; matrix products, arithmetic and copies ran while one was open for 16% of the time, Pallas kernels for 0%

commit v1 on v0

--- a/solution.py
+++ b/solution.py
@@ -4,6 +4,23 @@
 from jax.sharding import PartitionSpec as P
 
 eps_norm = 1e-05
+
+
+def joined_along(parts, dim):
+    dims = list(parts.shape[1:])
+    dims[dim] *= parts.shape[0]
+    return jnp.moveaxis(parts, 0, dim).reshape(dims)
+
+
+def collected_by_bits(x, axis):
+    size, index = (lax.axis_size(axis), lax.axis_index(axis))
+    pieces, bit = (x[None], 1)
+    while bit < size:
+        theirs = lax.ppermute(pieces, axis, [(i, i ^ bit) for i in range(size)])
+        low = index & bit == 0
+        pieces = jnp.concatenate([jnp.where(low, pieces, theirs), jnp.where(low, theirs, pieces)])
+        bit *= 2
+    return pieces
 
 
 def layer_norm_forward(values):
@@ -54,7 +71,7 @@
     left_projected = projected_rows[:, :, :projected_width]
     right_proj = projected_rows[:, :, projected_width:]
     live_rows = jnp.sum(sequence_mask.astype(jnp.float32))
-    right_all = lax.all_gather(right_proj, "res", axis=1, tiled=True)
+    right_all = joined_along(collected_by_bits(right_proj, "res"), 1)
     residue_count = right_all.shape[1]
     block_columns = 256 if residue_count % 256 == 0 else residue_count
     block_count = residue_count // block_columns

time: 90 us -> 114 us (1.27)
  waiting for transfers between devices: 14 us -> 64 us
  blocking collectives: 32.3 us -> 0 us
  starting transfers between devices: 0.04 us -> 7.98 us
  local copies, waits for them, and re-layouts: 13.8 us -> 8.91 us
  matrix products: 8.48 us -> 10.8 us
  other arithmetic: 6.82 us -> 8.18 us
    ppermute x0 -> x4, waiting for transfers between devices: none -> 34.7 us  [collected_by_bits(): theirs = lax.ppermute(pieces, axis, [(i, i ^ bit) for i in range(size)])]
    all_gather x1 -> x0, blocking collectives: 32.3 us -> none  [body(): right_all = lax.all_gather(right_proj, 'res', axis=1, tiled=True)]
    unnamed x2, waiting for transfers between devices: 14 us -> 29.3 us
    ppermute x0 -> x4, starting transfers between devices: none -> 7.94 us  [collected_by_bits(): theirs = lax.ppermute(pieces, axis, [(i, i ^ bit) for i in range(size)])]
    all_gather x2 -> x0, local copies, waits for them, and re-layouts: 6.35 us -> none  [body(): right_all = lax.all_gather(right_proj, 'res', axis=1, tiled=True)]
    dot_general x1, local copies, waits for them, and re-layouts: 1.74 us -> 0.15 us  [pair_block(): jnp.einsum('ijcd,sjd->sic', grad_outer, right_blk, preferred_element_type...]
    dot_general x1, matrix products: 0.81 us -> 2.38 us  [pair_block(): jnp.einsum('ijcd,sic->jsd', grad_outer, left_projected, preferred_element...]
    transpose x0 -> x1, local copies, waits for them, and re-layouts: none -> 1.38 us  [joined_along(): return jnp.moveaxis(parts, 0, dim).reshape(dims)]
  transfers between devices with their start and end apart: 1 -> 5, of which waited for: 1 -> 5; matrix products, arithmetic and copies ran while one was open for 16% -> 14% of each run, Pallas kernels for 0% -> 0%
where the time goes in v1:
time: 114 us
  waiting for transfers between devices  64 us (56%)
  between operations  14.2 us (12%)
  matrix products  10.8 us (9%)
  local copies, waits for them, and re-layouts  8.91 us (8%)
  other arithmetic  8.18 us (7%)
  starting transfers between devices  7.98 us (7%)
    ppermute x4, waiting for transfers between devices, collected_by_bits(): theirs = lax.ppermute(pieces, axis, [(i, i ^ bit) for i in range(size)])  34.7 us
    unnamed x2, waiting for transfers between devices  29.3 us
    ppermute x4, starting transfers between devices, collected_by_bits(): theirs = lax.ppermute(pieces, axis, [(i, i ^ bit) for i in range(size)])  7.94 us
    unnamed x16, local copies, waits for them, and re-layouts  2.53 us
    dot_general x1, matrix products, pair_block(): jnp.einsum('ijcd,sic->jsd', grad_outer, left_projected, preferred_element...  2.38 us
    dot_general x1, matrix products, pair_block(): jnp.einsum('ijcd,sjd->sic', grad_outer, right_blk, preferred_element_type...  2.31 us
  transfers between devices with their start and end apart: 5, of which 5 were waited for; matrix products, arithmetic and copies ran while one was open for 14% of the time, Pallas kernels for 0%

profile of v1, /device:TPU:0, one launch (start us, length us, event | category | flops | bytes accessed | tf_op | source)
XLA Modules:
  0.0 114.1 jit_solution(9521382975421033482)
XLA Ops:
  7.2 1.3 %convert_reduce_fusion.1 = f32[]{:T(128)} fusion(s32[64]{0:T(128)} %param.12), kind=kLoop, calls=%fused_computation.60 | loop fusion | flops 127 | bytes 260 | tf_op jit(solution)/shard_map/reduce_sum | solution.py:73
  8.5 0.7 convert_element_type.41
  9.2 0.7 convert_element_type.42
  9.8 1.1 convert_reduce_fusion
  10.9 1.2 %fusion.23 = f32[64,8]{1,0:T(8,128)S(1)} fusion(bf16[64,8,256]{2,1,0:T(8,128)(2,1)} %param.7, f32[64,8]{1,0:T(8,128)S(1)} %broadcast_multiply_fusion.3), kind=kLoop, calls=%fused_computation.29 | loop fusion | flops 523776 | bytes 266240 | tf_op jit(solution)/shard_map/reduce_sum | solution.py:29
  12.1 0.7 broadcast_multiply_fusion.4
  12.9 1.3 %fusion.9 = bf16[64,8,64]{2,1,0:T(8,128)(2,1)S(1)} fusion(bf16[64,8,256]{2,1,0:T(8,128)(2,1)} %param.7, f32[64,8]{1,0:T(8,128)S(1)} %get-tuple-element.47, f32[64,8]{1,0:T(8,128)S(1)} %broadcast_multiply_fusion.3, f32[64,8]{1,0:T(8,128)S(1)} %get-tuple-element.48, bf16[256,64]{0,1:T(8,128)(2,1)} %param.8), kind=kOutput, calls=%fused_computation.12 | convolution fusion | flops 17367040 | bytes 366592 | tf_op jit(solution)/shard_map/dot_general | solution.py:61
  14.3 0.6 collective-permute-start
  14.9 1.0 collective-permute-done
  16.1 2.9 %collective-permute-start.1 = (bf16[2,64,8,32]{3,2,1,0:T(8,128)(2,1)S(1)}, bf16[2,64,8,32]{3,2,1,0:T(8,128)(2,1)S(1)}, u32[]{:S(2)}, u32[]{:S(2)}) collective-permute-start(bf16[2,64,8,32]{3,2,1,0:T(8,128)(2,1)S(1)} %pad_maximum_fusion.2), channel_id=1, source_target_pairs={{0,2},{1,3},{2,0},{3,1},{4,6},{5,7},{6,4},{7,5},{8,10},{9,11},{10,... | collective-permute-start | bytes 196616 | tf_op jit(solution)/shard_map/ppermute | solution.py:19
  19.1 6.5 %collective-permute-done.1 = bf16[2,64,8,32]{3,2,1,0:T(8,128)(2,1)S(1)} collective-permute-done((bf16[2,64,8,32]{3,2,1,0:T(8,128)(2,1)S(1)}, bf16[2,64,8,32]{3,2,1,0:T(8,128)(2,1)S(1)}, u32[]{:S(2)}, u32[]{:S(2)}) %collective-permute-start.1) | collective-permute-done | bytes 65568 | tf_op jit(solution)/shard_map/ppermute | solution.py:19
  25.8 1.9 %collective-permute-start.2 = (bf16[4,64,8,32]{3,2,1,0:T(8,128)(2,1)S(1)}, bf16[4,64,8,32]{3,2,1,0:T(8,128)(2,1)S(1)}, u32[]{:S(2)}, u32[]{:S(2)}) collective-permute-start(bf16[4,64,8,32]{3,2,1,0:T(8,128)(2,1)S(1)} %pad_maximum_fusion.1), channel_id=1, source_target_pairs={{0,4},{1,5},{2,6},{3,7},{4,0},{5,1},{6,2},{7,3},{8,12},{9,13},{10,... | collective-permute-start | bytes 393224 | tf_op jit(solution)/shard_map/ppermute | solution.py:19
  27.7 2.0 %divide_convert_fusion = bf16[8,128,32,32]{1,3,2,0:T(8,128)(2,1)} fusion(bf16[32,32,128,1]{2,1,0,3:T(8,128)(2,1)S(1)} %bitcast.55, f32[8,128]{1,0:T(8,128)S(1)} %multiply_maximum_fusion, bf16[8,128,128]{2,1,0:T(8,128)(2,1)S(1)} %copy-done.5), kind=kOutput, calls=%fused_computation | convolution fusion | flops 270532608 | bytes 2625536 | tf_op jit(solution)/shard_map/while/body/eval_jaxpr/dot_general | solution.py:94
  29.8 9.4 %collective-permute-done.2 = bf16[4,64,8,32]{3,2,1,0:T(8,128)(2,1)S(1)} collective-permute-done((bf16[4,64,8,32]{3,2,1,0:T(8,128)(2,1)S(1)}, bf16[4,64,8,32]{3,2,1,0:T(8,128)(2,1)S(1)}, u32[]{:S(2)}, u32[]{:S(2)}) %collective-permute-start.2) | collective-permute-done | bytes 131104 | tf_op jit(solution)/shard_map/ppermute | solution.py:19
  39.6 0.6 copy.22
  40.3 2.6 %collective-permute-start.3 = (bf16[8,64,8,32]{1,3,2,0:T(8,128)(2,1)S(1)}, bf16[8,64,8,32]{1,3,2,0:T(8,128)(2,1)S(1)}, u32[]{:S(2)}, u32[]{:S(2)}) collective-permute-start(bf16[8,64,8,32]{1,3,2,0:T(8,128)(2,1)S(1)} %copy.22), channel_id=1, source_target_pairs={{0,8},{1,9},{2,10},{3,11},{4,12},{5,13},{6,14},{7,15},{8,0},{9,1},... | collective-permute-start | bytes 786440 | tf_op jit(solution)/shard_map/ppermute | solution.py:19
  42.9 2.4 %fusion.4 = f32[128,64,32]{0,1,2:T(8,128)S(1)} fusion(bf16[8,128,32,32]{1,3,2,0:T(8,128)(2,1)} %divide_convert_fusion, bf16[64,8,32]{0,2,1:T(8,128)(2,1)S(1)} %copy.27), kind=kOutput, calls=%fused_computation.7 | convolution fusion | flops 134217728 | bytes 3178496 | tf_op jit(solution)/shard_map/while/body/eval_jaxpr/ijcd,sic->jsd/dot_general | solution.py:105
  45.2 0.6 copy.34
  45.9 1.3 %copy.47 = f32[128,2048]{1,0:T(8,128)} copy(f32[128,2048]{0,1:T(8,128)S(1)} %bitcast.59) | data formatting | bytes 2097152
  47.2 17.8 %collective-permute-done.3 = bf16[8,64,8,32]{1,3,2,0:T(8,128)(2,1)S(1)} collective-permute-done((bf16[8,64,8,32]{1,3,2,0:T(8,128)(2,1)S(1)}, bf16[8,64,8,32]{1,3,2,0:T(8,128)(2,1)S(1)}, u32[]{:S(2)}, u32[]{:S(2)}) %collective-permute-start.3) | collective-permute-done | bytes 262176 | tf_op jit(solution)/shard_map/ppermute | solution.py:19
  65.0 0.6 copy.23
  65.9 0.4 maximum_bitcast_fusion
  66.3 1.4 %copy.25 = bf16[64,16,8,32]{0,3,2,1:T(8,128)(2,1)S(1)} copy(bf16[64,16,8,32]{3,2,0,1:T(8,128)(2,1)S(1)} %maximum_bitcast_fusion) | data formatting | bytes 1048576 | tf_op jit(solution)/shard_map/transpose | solution.py:12
  67.7 1.1 copy.30
  68.8 2.3 %fusion.10 = f32[64,8,32]{0,2,1:T(8,128)S(1)} fusion(bf16[8,128,32,32]{1,3,2,0:T(8,128)(2,1)} %divide_convert_fusion, bf16[64,128,32]{1,0,2:T(8,128)(2,1)S(1)} %copy.30), kind=kOutput, calls=%fused_computation.13 | convolution fusion | flops 134217728 | bytes 2686976 | tf_op jit(solution)/shard_map/while/body/eval_jaxpr/ijcd,sjd->sic/dot_general | solution.py:102
  71.3 0.7 convert_bitcast_fusion
  72.0 1.4 %copy.28 = bf16[8,128,32,32]{1,3,2,0:T(8,128)(2,1)S(1)} copy(bf16[8,128,32,32]{1,2,0,3:T(8,128)(2,1)S(1)} %convert_bitcast_fusion) | data formatting | bytes 4194304 | tf_op jit(solution)/shard_map/while/body/eval_jaxpr/convert_element_type | solution.py:89
  73.4 1.5 %fusion.8 = bf16[8,128,128]{2,1,0:T(8,128)(2,1)} fusion(bf16[8,128,1024]{1,2,0:T(8,128)(2,1)S(1)} %bitcast.60, bf16[1024,128]{1,0:T(8,128)(2,1)S(1)} %copy-done, f32[8,128]{1,0:T(8,128)S(1)} %multiply_maximum_fusion, f32[128]{0:T(128)S(1)} %copy-done.6), kind=kOutput, calls=%fused_computation.10 | convolution fusion | flops 268828672 | bytes 2626048 | tf_op jit(solution)/shard_map/while/body/eval_jaxpr/dot_general | solution.py:90
  74.9 29.3 %reduce-scatter.4.cloned.1.call-done = f32[8,2048]{1,0:T(8,128)} async-done(((f32[128,2048]{1,0:T(8,128)}), f32[8,2048]{1,0:T(8,128)}) %reduce-scatter.4.cloned.1.call-update) | async-done | bytes 65552
  104.2 1.2 %copy.48 = f32[8,2048]{0,1:T(8,128)S(1)} copy(f32[8,2048]{1,0:T(8,128)} %reduce-scatter.4.cloned.1.call-done) | data formatting | bytes 131072
  105.7 0.5 fusion.39
  106.2 1.0 fusion.22
  (32 shorter events, 1.9 us)
Async XLA Ops:
  7.2 20.5 %copy-start = (bf16[1024,128]{1,0:T(8,128)(2,1)S(1)}, bf16[1024,128]{1,0:T(8,128)(2,1)}, u32[]{:S(2)}) copy-start(bf16[1024,128]{1,0:T(8,128)(2,1)} %param.9) | copy-start | bytes 786436
  7.2 97.0 %reduce-scatter.4.cloned.1.call-start = ((), (), s32[]{:S(2)}) async-start(), calls=%async_computation.1 | async-start | bytes 1114112
  12.9 2.0 %copy-start.2 = (f32[64,8]{1,0:T(8,128)}, f32[64,8]{1,0:T(8,128)S(1)}, u32[]{:S(2)}) copy-start(f32[64,8]{1,0:T(8,128)S(1)} %get-tuple-element.48) | copy-start | bytes 6148
  14.2 13.4 %copy-start.5 = (bf16[8,128,128]{2,1,0:T(8,128)(2,1)S(1)}, bf16[8,128,128]{2,1,0:T(8,128)(2,1)}, u32[]{:S(2)}) copy-start(bf16[8,128,128]{2,1,0:T(8,128)(2,1)} %param.11) | copy-start | bytes 786436
  14.3 1.5 %collective-permute-start = (bf16[1,64,8,32]{3,2,1,0:T(8,128)(2,1)S(1)}, bf16[1,64,8,32]{3,2,1,0:T(8,128)(2,1)S(1)}, u32[]{:S(2)}, u32[]{:S(2)}) collective-permute-start(bf16[1,64,8,32]{3,2,1,0:T(8,128)(2,1)S(1)} %get-tuple-element.45), channel_id=1, source_target_pairs={{0,1},{1,0},{2,3},{3,2},{4,5},{5,4},{6,7},{7,6},{8,9},{9,8},{10,11... | collective-permute-start | bytes 98312 | tf_op jit(solution)/shard_map/ppermute | solution.py:19
  16.1 9.5 %collective-permute-start.1 = (bf16[2,64,8,32]{3,2,1,0:T(8,128)(2,1)S(1)}, bf16[2,64,8,32]{3,2,1,0:T(8,128)(2,1)S(1)}, u32[]{:S(2)}, u32[]{:S(2)}) collective-permute-start(bf16[2,64,8,32]{3,2,1,0:T(8,128)(2,1)S(1)} %pad_maximum_fusion.2), channel_id=1, source_target_pairs={{0,2},{1,3},{2,0},{3,1},{4,6},{5,7},{6,4},{7,5},{8,10},{9,11},{10,... | collective-permute-start | bytes 196616 | tf_op jit(solution)/shard_map/ppermute | solution.py:19
  25.8 13.5 %collective-permute-start.2 = (bf16[4,64,8,32]{3,2,1,0:T(8,128)(2,1)S(1)}, bf16[4,64,8,32]{3,2,1,0:T(8,128)(2,1)S(1)}, u32[]{:S(2)}, u32[]{:S(2)}) collective-permute-start(bf16[4,64,8,32]{3,2,1,0:T(8,128)(2,1)S(1)} %pad_maximum_fusion.1), channel_id=1, source_target_pairs={{0,4},{1,5},{2,6},{3,7},{4,0},{5,1},{6,2},{7,3},{8,12},{9,13},{10,... | collective-permute-start | bytes 393224 | tf_op jit(solution)/shard_map/ppermute | solution.py:19
  40.3 24.7 %collective-permute-start.3 = (bf16[8,64,8,32]{1,3,2,0:T(8,128)(2,1)S(1)}, bf16[8,64,8,32]{1,3,2,0:T(8,128)(2,1)S(1)}, u32[]{:S(2)}, u32[]{:S(2)}) collective-permute-start(bf16[8,64,8,32]{1,3,2,0:T(8,128)(2,1)S(1)} %copy.22), channel_id=1, source_target_pairs={{0,8},{1,9},{2,10},{3,11},{4,12},{5,13},{6,14},{7,15},{8,0},{9,1},... | collective-permute-start | bytes 786440 | tf_op jit(solution)/shard_map/ppermute | solution.py:19
  72.0 1.4 %copy-start.6 = (f32[128]{0:T(128)S(1)}, f32[128]{0:T(128)}, u32[]{:S(2)}) copy-start(f32[128]{0:T(128)} %param.10) | copy-start | bytes 1540
  74.9 30.8 %copy-start.1 = (bf16[64,8,256]{2,1,0:T(8,128)(2,1)S(1)}, bf16[64,8,256]{2,1,0:T(8,128)(2,1)}, u32[]{:S(2)}) copy-start(bf16[64,8,256]{2,1,0:T(8,128)(2,1)} %param.7) | copy-start | bytes 786436
  74.9 30.8 %copy-start.3 = (f32[64,8]{1,0:T(8,128)S(1)}, f32[64,8]{1,0:T(8,128)}, u32[]{:S(2)}) copy-start(f32[64,8]{1,0:T(8,128)} %copy-done.2) | copy-start | bytes 6148
  74.9 30.8 %copy-start.4 = (bf16[256,64]{0,1:T(8,128)(2,1)S(1)}, bf16[256,64]{0,1:T(8,128)(2,1)}, u32[]{:S(2)}) copy-start(bf16[256,64]{0,1:T(8,128)(2,1)} %param.8) | copy-start | bytes 98308
Sparse Core Ops, SparseCore 0:
  47.3 56.7 reduce-scatter.3
